TPU v7x, 32 devices: a whole 2x2x4 slice. The times are simulated.
32 devices in a mesh: member: 4 (over y, x), space: 8 (over z, core).
Axes of the slice: x: 2, y: 2, z: 4, core: 2. Of those that a mesh axis runs over, the one named last changes fastest.
Arguments:
- features: bfloat16 [8, 32, 64, 1024], P('member', None, 'space'), may hold values from -6 to 6
- skip: bfloat16 [8, 32, 64, 1024], P('member', None, 'space'), may hold values from -6 to 6
- conv_weight: bfloat16 [3, 3, 32, 32], replicated, may hold values from -0.625 to 0.625
- out_weight: bfloat16 [2, 32], replicated, may hold values from -2 to 2
- target: float32 [2, 64, 1024], P(None, 'space'), may hold values from -12 to 12
Outputs:
- grad_input: bfloat16 [8, 32, 64, 1024], P('member', None, 'space')
All inputs are finite; a program needn't handle non-finite values.
Results may differ from a plain program's by a relative error of at most 0.012.
Values may be sent and summed in bfloat16 or wider, within the bound.
A program may use at most 64 MiB of HBM per device.

v0:
```python
import math

import jax
import jax.numpy as jnp
from jax import lax
from jax.sharding import PartitionSpec as P

root_coef = math.sqrt(2.0 / math.pi)
cubic_coef = 0.044715
smooth = 0.25


def extended(cells, sides, width):
    for axis, dim in sides:
        count = lax.axis_size(axis)
        ends = count - 1
        head = lax.slice_in_dim(cells, 0, width, axis=dim)
        tail = lax.slice_in_dim(cells, cells.shape[dim] - width, cells.shape[dim], axis=dim)
        cells = jnp.concatenate(
            [
                lax.ppermute(tail, axis, [(i, (i + 1) % count) for i in range(ends)]),
                cells,
                lax.ppermute(head, axis, [((i + 1) % count, i) for i in range(ends)]),
            ],
            axis=dim,
        )
    return cells


def gelu_value(source):
    inside = root_coef * (source + cubic_coef * source * source * source)
    return 0.5 * source * (1.0 + jnp.tanh(inside))


def gelu_slope(source):
    inside = root_coef * (source + cubic_coef * source * source * source)
    tanh_val = jnp.tanh(inside)
    return 0.5 * (1.0 + tanh_val) + 0.5 * source * (1.0 - tanh_val * tanh_val) * root_coef * (
        1.0 + 3.0 * cubic_coef * source * source
    )


def smooth_slope(source):
    return source / jnp.sqrt(source * source + smooth * smooth)


def tap_sum(source, weight, flipped):
    row_count = source.shape[2] - 2
    col_count = source.shape[3]
    padded = jnp.pad(source, ((0, 0), (0, 0), (0, 0), (1, 1)))
    if flipped:
        matrix = jnp.transpose(weight, (3, 0, 1, 2)).reshape(weight.shape[3], -1)
    else:
        matrix = jnp.transpose(weight, (2, 0, 1, 3)).reshape(weight.shape[2], -1)
    results = []
    for member_at in range(source.shape[0]):
        pieces = []
        for row_tap in range(3):
            for col_tap in range(3):
                row_at = 2 - row_tap if flipped else row_tap
                col_at = 2 - col_tap if flipped else col_tap
                pieces.append(
                    padded[member_at, :, row_at : row_at + row_count, col_at : col_at + col_count]
                )
        stacked = jnp.concatenate(pieces, axis=0)
        results.append(
            jnp.einsum("ok,krw->orw", matrix, stacked, preferred_element_type=jnp.float32)
        )
    return jnp.stack(results, axis=0)


def local(features, skip, conv_weight, out_weight, target):
    haloed = extended(features, (("space", 2),), 1)
    preact = tap_sum(haloed, conv_weight, False) + skip.astype(jnp.float32)
    active = gelu_value(preact).astype(jnp.bfloat16)
    outputs = jnp.einsum("ko,morw->mkrw", out_weight, active, preferred_element_type=jnp.float32)
    all_members = lax.all_gather(outputs, "member", axis=0, tiled=True)
    member_total = all_members.shape[0]
    pair_term = jnp.sum(smooth_slope(outputs[:, None] - all_members[None, :]), axis=1)
    grad_out = (smooth_slope(outputs - target[None]) - pair_term / (member_total - 1)).astype(
        jnp.bfloat16
    )
    grad_active = jnp.einsum(
        "ko,mkrw->morw", out_weight, grad_out, preferred_element_type=jnp.float32
    )
    grad_preact = (grad_active * gelu_slope(preact)).astype(jnp.bfloat16)
    grad_haloed = extended(grad_preact, (("space", 2),), 1)
    return tap_sum(grad_haloed, conv_weight, True).astype(jnp.bfloat16)


def solution(mesh):
    placed = (
        P("member", None, "space", None),
        P("member", None, "space", None),
        P(),
        P(),
        P(None, "space", None),
    )
    return jax.shard_map(
        local,
        mesh=mesh,
        in_specs=placed,
        out_specs=P("member", None, "space", None),
        check_vma=False,
    )
```

profile of v0, /device:TPU:1, one launch (start us, length us, event | category | flops | bytes accessed | tf_op | source)
XLA Modules:
  0.0 48.1 jit_solution(13501318715697524126)
XLA Ops:
  0.0 0.0 copy-start
  0.0 1.8 %copy.66 = bf16[2,32,8,1024]{3,1,2,0:T(8,128)(2,1)S(1)} copy(bf16[2,32,8,1024]{3,2,1,0:T(8,128)(2,1)} %param.5) | data formatting | bytes 2097152 | tf_op args[0]
  1.8 4.6 %collective-permute-start = (bf16[2,32,1,1024]{3,1,2,0:T(8,128)(2,1)S(1)}, bf16[2,32,1,1024]{3,1,2,0:T(8,128)(2,1)S(1)}, u32[]{:S(2)}, u32[]{:S(2)}) collective-permute-start(bf16[2,32,1,1024]{3,1,2,0:T(8,128)(2,1)S(1)} %get-tuple-element.29), channel_id=1, source_target_pairs={{0,1},{1,2},{2,3},{3,4},{4,5},{5,6},{6,7},{8,9},{9,10},{10,11},{11... | collective-permute-start | bytes 393224 | tf_op jit(solution)/shard_map/ppermute | solution.py:21
  6.4 1.9 %collective-permute-start.1 = (bf16[2,32,1,1024]{3,1,2,0:T(8,128)(2,1)S(1)}, bf16[2,32,1,1024]{3,1,2,0:T(8,128)(2,1)S(1)}, u32[]{:S(2)}, u32[]{:S(2)}) collective-permute-start(bf16[2,32,1,1024]{3,1,2,0:T(8,128)(2,1)S(1)} %get-tuple-element.30), channel_id=1, source_target_pairs={{1,0},{2,1},{3,2},{4,3},{5,4},{6,5},{7,6},{9,8},{10,9},{11,10},{12... | collective-permute-start | bytes 393224 | tf_op jit(solution)/shard_map/ppermute | solution.py:23
  8.4 0.9 %copy.72 = bf16[32,3,3,32]{3,2,1,0:T(4,128)(2,1)S(1)} copy(bf16[32,3,3,32]{3,0,2,1:T(8,128)(2,1)} %bitcast.191) | data formatting | bytes 36864 | tf_op jit(solution)/shard_map/transpose | solution.py:54
  9.3 0.1 reshape.11
  9.4 0.0 collective-permute-done
  9.5 1.8 %constant_dynamic-update-slice_fusion.3 = (bf16[2,32,9,1024]{3,1,2,0:T(8,128)(2,1)S(1)}, bf16[2,32,9,1024]{3,1,2,0:T(8,128)(2,1)S(1)}) fusion(bf16[2,32,8,1024]{3,2,1,0:T(8,128)(2,1)} %param.5, bf16[2,32,9,1024]{3,1,2,0:T(8,128)(2,1)S(1)} %constant_dynamic-update-slice_fusion.1), kind=kLoop, calls=%fused_computation.114 | loop fusion | bytes 3145728
  11.3 1.4 %collective-permute-done.1 = bf16[2,32,1,1024]{3,1,2,0:T(8,128)(2,1)S(1)} collective-permute-done((bf16[2,32,1,1024]{3,1,2,0:T(8,128)(2,1)S(1)}, bf16[2,32,1,1024]{3,1,2,0:T(8,128)(2,1)S(1)}, u32[]{:S(2)}, u32[]{:S(2)}) %collective-permute-start.1) | collective-permute-done | bytes 131104 | tf_op jit(solution)/shard_map/ppermute | solution.py:23
  12.7 0.8 %fusion.12 = bf16[2,32,10,1026]{3,1,2,0:T(8,128)(2,1)S(1)} fusion(bf16[2,32,1,1024]{3,1,2,0:T(8,128)(2,1)S(1)} %collective-permute-done.1, bf16[2,32,8,1024]{3,1,2,0:T(8,128)(2,1)S(1)} %copy.66, bf16[2,32,1,1024]{3,1,2,0:T(8,128)(2,1)S(1)} %collective-permute-done), kind=kLoop, calls=%fused_computation.22 | loop fusion | flops 7879680 | bytes 2624000 | tf_op jit(solution)/shard_map/concatenate | solution.py:19
  13.6 0.1 fusion.57
  13.7 0.3 fusion.55
  14.0 0.3 fusion.54
  14.3 0.3 fusion.52
  14.6 0.3 fusion.51
  14.9 0.3 fusion.49
  15.2 0.2 fusion.40
  15.5 0.0 copy-start.3
  15.5 1.0 %convolution_bitcast_fusion.1 = f32[1,32,8,1024]{3,1,2,0:T(8,128)S(1)} fusion(bf16[32,288,1]{1,0,2:T(8,128)(2,1)S(1)} %reshape.11, bf16[288,8,1024]{2,0,1:T(8,128)(2,1)S(1)} %get-tuple-element.15), kind=kOutput, calls=%fused_computation.24 | convolution fusion | flops 150994944 | bytes 5785600 | tf_op jit(solution)/shard_map/ok,krw->orw/dot_general | solution.py:67
  16.4 1.0 %convolution_bitcast_fusion = f32[1,32,8,1024]{3,1,2,0:T(8,128)S(1)} fusion(bf16[32,288,1]{1,0,2:T(8,128)(2,1)S(1)} %reshape.11, bf16[288,8,1024]{2,0,1:T(8,128)(2,1)S(1)} %fusion.40), kind=kOutput, calls=%fused_computation.23 | convolution fusion | flops 150994944 | bytes 5785600 | tf_op jit(solution)/shard_map/ok,krw->orw/dot_general | solution.py:67
  17.4 0.0 copy-done
  17.4 0.0 copy-done.3
  17.5 0.0 copy-start.2
  17.5 1.2 %fusion.18 = f32[2,8,1024,2]{2,3,1,0:T(2,128)S(1)} fusion(f32[1,32,8,1024]{3,1,2,0:T(8,128)S(1)} %convolution_bitcast_fusion, f32[1,32,8,1024]{3,1,2,0:T(8,128)S(1)} %convolution_bitcast_fusion.1, bf16[2,32,8,1024]{3,2,1,0:T(8,128)(2,1)S(1)} %copy-done.3, bf16[2,32]{1,0:T(2,128)(2,1)S(1)} %copy-done), kind=kOutput, calls=%fused_computation.33 | convolution fusion | flops 8388608 | bytes 3276928 | tf_op jit(solution)/shard_map/ko,morw->mkrw/dot_general | solution.py:76
  18.7 8.2 %all_gather.3 = f32[8,2,8,1024]{3,2,1,0:T(8,128)S(1)} all-gather(f32[2,2,8,1024]{3,2,1,0:T(8,128)S(1)} %bitcast.189), channel_id=1, replica_groups=mesh['member'=4,'space'=8] {'member'}, dimensions={0}, use_global_device_ids=true | all-gather | bytes 655360 | tf_op jit(solution)/shard_map/all_gather | solution.py:77
  26.9 0.2 fusion.17
  27.1 0.0 copy-done.2
  27.1 0.1 subtract_convert_fusion
  27.2 2.0 %fusion.7 = bf16[2,32,8,1024]{3,1,2,0:T(8,128)(2,1)S(1)} fusion(f32[1,32,8,1024]{3,1,2,0:T(8,128)S(1)} %convolution_bitcast_fusion, f32[1,32,8,1024]{3,1,2,0:T(8,128)S(1)} %convolution_bitcast_fusion.1, bf16[2,32,8,1024]{3,2,1,0:T(8,128)(2,1)S(1)} %copy-done.3, bf16[2,2,8,1024]{3,2,1,0:T(8,128)(2,1)S(1)} %subtract_convert_fusion, bf16[2,32]{1,0:T(2,128)(2,1)S(1)} %copy-done), kind=kOutput, calls=%fused_computation.11 | convolution fusion | flops 13631488 | bytes 4259968 | tf_op jit(solution)/shard_map/ko,mkrw->morw/dot_general | solution.py:83
  29.2 5.3 %collective-permute-start.2 = (bf16[2,32,1,1024]{3,1,2,0:T(8,128)(2,1)S(1)}, bf16[2,32,1,1024]{3,1,2,0:T(8,128)(2,1)S(1)}, u32[]{:S(2)}, u32[]{:S(2)}) collective-permute-start(bf16[2,32,1,1024]{3,1,2,0:T(8,128)(2,1)S(1)} %get-tuple-element.25), channel_id=1, source_target_pairs={{0,1},{1,2},{2,3},{3,4},{4,5},{5,6},{6,7},{8,9},{9,10},{10,11},{11... | collective-permute-start | bytes 393224 | tf_op jit(solution)/shard_map/ppermute | solution.py:21
  34.5 2.1 %collective-permute-start.3 = (bf16[2,32,1,1024]{3,1,2,0:T(8,128)(2,1)S(1)}, bf16[2,32,1,1024]{3,1,2,0:T(8,128)(2,1)S(1)}, u32[]{:S(2)}, u32[]{:S(2)}) collective-permute-start(bf16[2,32,1,1024]{3,1,2,0:T(8,128)(2,1)S(1)} %get-tuple-element.26), channel_id=1, source_target_pairs={{1,0},{2,1},{3,2},{4,3},{5,4},{6,5},{7,6},{9,8},{10,9},{11,10},{12... | collective-permute-start | bytes 393224 | tf_op jit(solution)/shard_map/ppermute | solution.py:23
  36.6 0.0 collective-permute-done.2
  36.6 4.2 %collective-permute-done.3 = bf16[2,32,1,1024]{3,1,2,0:T(8,128)(2,1)S(1)} collective-permute-done((bf16[2,32,1,1024]{3,1,2,0:T(8,128)(2,1)S(1)}, bf16[2,32,1,1024]{3,1,2,0:T(8,128)(2,1)S(1)}, u32[]{:S(2)}, u32[]{:S(2)}) %collective-permute-start.3) | collective-permute-done | bytes 131104 | tf_op jit(solution)/shard_map/ppermute | solution.py:23
  40.8 0.8 %select_maximum_fusion = bf16[2,32,10,1026]{3,1,2,0:T(8,128)(2,1)S(1)} fusion(bf16[2,32,1,1024]{3,1,2,0:T(8,128)(2,1)S(1)} %collective-permute-done.3, bf16[2,32,8,1024]{3,1,2,0:T(8,128)(2,1)S(1)} %fusion.7, bf16[2,32,1,1024]{3,1,2,0:T(8,128)(2,1)S(1)} %collective-permute-done.2), kind=kLoop, calls=%fused_computation.16 | loop fusion | flops 7879680 | bytes 2624000 | tf_op jit(solution)/shard_map/concatenate | solution.py:19
  41.6 0.2 fusion.39
  41.9 0.3 fusion.37
  42.2 0.3 fusion.36
  42.5 0.3 fusion.34
  42.8 0.0 copy-start.1
  42.9 0.3 fusion.33
  43.2 0.3 fusion.31
  43.5 0.1 fusion.20
  43.5 0.1 copy-done.1
  43.7 1.4 %fusion.13 = bf16[1,32,8,1024]{3,1,2,0:T(8,128)(2,1)S(1)} fusion(bf16[288,8,1024]{2,0,1:T(8,128)(2,1)S(1)} %get-tuple-element.5, bf16[32,288,1]{0,1,2:T(8,128)(2,1)S(1)} %bitcast.192), kind=kOutput, calls=%fused_computation.27 | convolution fusion | flops 151257088 | bytes 5261312 | tf_op jit(solution)/shard_map/ok,krw->orw/dot_general | solution.py:67
  45.1 1.4 %fusion.14 = bf16[1,32,8,1024]{3,1,2,0:T(8,128)(2,1)S(1)} fusion(bf16[288,8,1024]{2,0,1:T(8,128)(2,1)S(1)} %fusion.20, bf16[32,288,1]{0,1,2:T(8,128)(2,1)S(1)} %bitcast.193), kind=kOutput, calls=%fused_computation.28 | convolution fusion | flops 151257088 | bytes 5261312 | tf_op jit(solution)/shard_map/ok,krw->orw/dot_general | solution.py:67
  46.4 0.1 pad_maximum_fusion
  46.5 1.5 %copy.79 = bf16[2,32,8,1024]{3,2,1,0:T(8,128)(2,1)} copy(bf16[2,32,8,1024]{3,1,2,0:T(8,128)(2,1)S(1)} %pad_maximum_fusion) | data formatting | bytes 2097152 | tf_op jit(solution)/shard_map/stack | solution.py:69
  (17 shorter events, 0.5 us)
Async XLA Ops:
  0.0 17.4 %copy-start = (bf16[2,32]{1,0:T(2,128)(2,1)S(1)}, bf16[2,32]{1,0:T(2,128)(2,1)}, u32[]{:S(2)}) copy-start(bf16[2,32]{1,0:T(2,128)(2,1)} %param.8) | copy-start | bytes 388
  1.8 7.6 %collective-permute-start = (bf16[2,32,1,1024]{3,1,2,0:T(8,128)(2,1)S(1)}, bf16[2,32,1,1024]{3,1,2,0:T(8,128)(2,1)S(1)}, u32[]{:S(2)}, u32[]{:S(2)}) collective-permute-start(bf16[2,32,1,1024]{3,1,2,0:T(8,128)(2,1)S(1)} %get-tuple-element.29), channel_id=1, source_target_pairs={{0,1},{1,2},{2,3},{3,4},{4,5},{5,6},{6,7},{8,9},{9,10},{10,11},{11... | collective-permute-start | bytes 393224 | tf_op jit(solution)/shard_map/ppermute | solution.py:21
  6.4 6.3 %collective-permute-start.1 = (bf16[2,32,1,1024]{3,1,2,0:T(8,128)(2,1)S(1)}, bf16[2,32,1,1024]{3,1,2,0:T(8,128)(2,1)S(1)}, u32[]{:S(2)}, u32[]{:S(2)}) collective-permute-start(bf16[2,32,1,1024]{3,1,2,0:T(8,128)(2,1)S(1)} %get-tuple-element.30), channel_id=1, source_target_pairs={{1,0},{2,1},{3,2},{4,3},{5,4},{6,5},{7,6},{9,8},{10,9},{11,10},{12... | collective-permute-start | bytes 393224 | tf_op jit(solution)/shard_map/ppermute | solution.py:23
  15.5 2.0 %copy-start.3 = (bf16[2,32,8,1024]{3,2,1,0:T(8,128)(2,1)S(1)}, bf16[2,32,8,1024]{3,2,1,0:T(8,128)(2,1)}, u32[]{:S(2)}) copy-start(bf16[2,32,8,1024]{3,2,1,0:T(8,128)(2,1)} %param.6) | copy-start | bytes 3145732
  17.5 9.7 %copy-start.2 = (f32[2,8,1024]{2,1,0:T(8,128)S(1)}, f32[2,8,1024]{2,1,0:T(8,128)}, u32[]{:S(2)}) copy-start(f32[2,8,1024]{2,1,0:T(8,128)} %param.9) | copy-start | bytes 196612
  29.2 7.4 %collective-permute-start.2 = (bf16[2,32,1,1024]{3,1,2,0:T(8,128)(2,1)S(1)}, bf16[2,32,1,1024]{3,1,2,0:T(8,128)(2,1)S(1)}, u32[]{:S(2)}, u32[]{:S(2)}) collective-permute-start(bf16[2,32,1,1024]{3,1,2,0:T(8,128)(2,1)S(1)} %get-tuple-element.25), channel_id=1, source_target_pairs={{0,1},{1,2},{2,3},{3,4},{4,5},{5,6},{6,7},{8,9},{9,10},{10,11},{11... | collective-permute-start | bytes 393224 | tf_op jit(solution)/shard_map/ppermute | solution.py:21
  34.5 6.3 %collective-permute-start.3 = (bf16[2,32,1,1024]{3,1,2,0:T(8,128)(2,1)S(1)}, bf16[2,32,1,1024]{3,1,2,0:T(8,128)(2,1)S(1)}, u32[]{:S(2)}, u32[]{:S(2)}) collective-permute-start(bf16[2,32,1,1024]{3,1,2,0:T(8,128)(2,1)S(1)} %get-tuple-element.26), channel_id=1, source_target_pairs={{1,0},{2,1},{3,2},{4,3},{5,4},{6,5},{7,6},{9,8},{10,9},{11,10},{12... | collective-permute-start | bytes 393224 | tf_op jit(solution)/shard_map/ppermute | solution.py:23
  42.8 0.9 %copy-start.1 = (bf16[3,3,32,32]{3,2,1,0:T(8,128)(2,1)S(1)}, bf16[3,3,32,32]{3,2,1,0:T(8,128)(2,1)}, u32[]{:S(2)}) copy-start(bf16[3,3,32,32]{3,2,1,0:T(8,128)(2,1)} %param.7) | copy-start | bytes 55300
where the time goes:
time: 48.4 us; the launch traced here: 48.1 us
  starting transfers between devices  13.9 us (29%)
  local copies, waits for them, and re-layouts  9.96 us (21%)
  blocking collectives  8.22 us (17%)
  matrix products  7.85 us (16%)
  waiting for transfers between devices  5.6 us (12%)
  other arithmetic  2.16 us (4%)
    ppermute x2, starting transfers between devices, extended(): lax.ppermute(tail, axis, [(i, (i + 1) % count) for i in range(ends)])  9.87 us
    all_gather x1, blocking collectives, local(): all_members = lax.all_gather(outputs, 'member', axis=0, tiled=True)  8.22 us
    unnamed x29, local copies, waits for them, and re-layouts  6.47 us
    ppermute x2, waiting for transfers between devices, extended(): lax.ppermute(head, axis, [((i + 1) % count, i) for i in range(ends)])  5.6 us
    dot_general x4, matrix products, tap_sum(): jnp.einsum('ok,krw->orw', matrix, stacked, preferred_element_type=jnp.flo...  4.69 us
    ppermute x2, starting transfers between devices, extended(): lax.ppermute(head, axis, [((i + 1) % count, i) for i in range(ends)])  4.02 us
    dot_general x1, matrix products, local(): jnp.einsum('ko,mkrw->morw', out_weight, grad_out, preferred_element_type=...  1.98 us
    concatenate x2, other arithmetic, extended(): jnp.concatenate([lax.ppermute(tail, axis, [(i, (i + 1) % count) for i in...  1.64 us
  transfers between devices with their start and end apart: 4, of which 2 were waited for; matrix products, arithmetic and copies ran while one was open for 6% of the time, Pallas kernels for 0%

commit v1 on v0

v1 whole, which is shorter than its diff:
```python
import functools
import math

import jax
import jax.numpy as jnp
from jax import lax
from jax.experimental import pallas as pl
from jax.experimental.pallas import tpu as pltpu
from jax.sharding import PartitionSpec as P

root_coef = math.sqrt(2.0 / math.pi)
cubic_coef = 0.044715
smooth = 0.25
MESH = pl.DeviceIdType.MESH
F32 = jnp.float32
BF16 = jnp.bfloat16


def gelu_value(source):
    inside = root_coef * (source + cubic_coef * source * source * source)
    return 0.5 * source * (1.0 + jnp.tanh(inside))


def gelu_slope(source):
    square = source * source
    tanh_val = jnp.tanh(root_coef * (source + cubic_coef * square * source))
    return 0.5 * (1.0 + tanh_val) + 0.5 * source * (1.0 - tanh_val * tanh_val) * (
        root_coef * (1.0 + 3.0 * cubic_coef * square)
    )


def smooth_slope(source):
    return source * lax.rsqrt(source * source + smooth * smooth)


def dot(left, right):
    return lax.dot_general(left, right, (((1,), (0,)), ((), ())), preferred_element_type=F32)


def dot_nt(left, right):
    return lax.dot_general(left, right, (((1,), (1,)), ((), ())), preferred_element_type=F32)


def split_index(shape, dim, size):
    index = lax.broadcasted_iota(jnp.int32, shape, dim)
    if size & (size - 1) == 0:
        return lax.shift_right_logical(index, size.bit_length() - 1), index & (size - 1)
    return lax.div(index, size), lax.rem(index, size)


def shifted(value, step):
    count = value.shape[1]
    edge = jnp.zeros((value.shape[0], 1), value.dtype)
    if step == 1:
        return jnp.concatenate([value[:, 1:], edge], axis=1)
    return jnp.concatenate([edge, value[:, : count - 1]], axis=1)


def kernel(
    dims, x_hbm, skip_hbm, weight, out_w, target_hbm, out_hbm,
    x, skip, target, stk, hstk, pre, act, hs, hx, gs, hg, outs, ybuf, gsend, gout,
    wf, wfh, wb, wbh, wo, wot, sel, obuf,
    in_sem, out_sem, hs_sem, hx_sem, gs_sem, hg_sem, as_sem, ar_sem, bs_sem, br_sem,
):
    members, chans, rows, cols, peers, count, outn, chunk = dims
    full = chans * rows
    wide = cols // peers
    me = lax.axis_index("member")
    at = lax.axis_index("space")
    has_up = at > 0
    has_dn = at < count - 1
    up = {"space": lax.max(at - 1, 0)}
    dn = {"space": lax.min(at + 1, count - 1)}
    mine = pl.ds(pl.multiple_of(me * wide, wide), wide)

    loads = [pltpu.make_async_copy(x_hbm.at[m], x.at[m], in_sem.at[m]) for m in range(members)]
    skips = [
        pltpu.make_async_copy(skip_hbm.at[m], skip.at[m], in_sem.at[members + m])
        for m in range(members)
    ]
    tgt = pltpu.make_async_copy(target_hbm.at[:, mine], target, in_sem.at[2 * members])
    for c in loads + skips + [tgt]:
        c.start()

    barrier = pltpu.get_barrier_semaphore()
    for d in range(1, peers):
        pl.semaphore_signal(
            barrier, inc=1, device_id={"member": lax.rem(me + d, peers)}, device_id_type=MESH
        )

    @pl.when(has_up)
    def _():
        pl.semaphore_signal(barrier, inc=1, device_id=up, device_id_type=MESH)

    @pl.when(has_dn)
    def _():
        pl.semaphore_signal(barrier, inc=1, device_id=dn, device_id_type=MESH)

    chan, row = split_index((2 * chans, full), 1, rows)
    half, pick = split_index((2 * chans, full), 0, chans)
    sel[...] = (
        (chan == pick) & (row == jnp.where(half == 0, 0, rows - 1))
    ).astype(F32).astype(BF16)

    left_chan, left_row = split_index((full, chans), 0, rows)
    spread = (left_chan == lax.broadcasted_iota(jnp.int32, (full, chans), 1)).astype(F32)
    spread = spread.astype(BF16)
    _, row_a = split_index((full, full), 0, rows)
    _, row_b = split_index((full, full), 1, rows)
    gap = row_b - row_a

    def place(slot):
        shape = (chans, 6 * chans)
        return (
            lax.broadcasted_iota(jnp.int32, shape, 1)
            == lax.broadcasted_iota(jnp.int32, shape, 0) + slot * chans
        ).astype(F32).astype(BF16)

    def build(main, halo, flipped):
        edges = jnp.zeros((full, 6 * chans), F32)
        for dc in range(3):
            band = jnp.zeros((full, full), F32)
            for dr in range(3):
                tap = weight[dr, dc]
                part = (dot_nt if flipped else dot)(spread, tap).astype(BF16)
                offset = 1 - dr if flipped else dr - 1
                band = jnp.where(gap == offset, dot_nt(part, spread), band)
                if offset != 0:
                    kept = jnp.where(
                        left_row == (0 if offset < 0 else rows - 1), part.astype(F32), 0.0
                    ).astype(BF16)
                    edges = edges + dot(kept, place(2 * dc + (0 if offset < 0 else 1)))
            main[:, dc * full : (dc + 1) * full] = band.astype(BF16)
        halo[...] = edges.astype(BF16)

    build(wf, wfh, False)

    out_k, _ = split_index((outn * rows, chans), 0, rows)
    lines = jnp.zeros((outn * rows, chans), F32)
    for k in range(outn):
        lines = jnp.where(out_k == k, out_w[k : k + 1, :].astype(F32), lines)
    lines = lines.astype(BF16)
    _, oa = split_index((outn * rows, full), 0, rows)
    _, ob = split_index((outn * rows, full), 1, rows)
    wo[...] = jnp.where(oa == ob, dot_nt(lines, spread), 0.0).astype(BF16)
    _, ta = split_index((full, outn * rows), 0, rows)
    _, tb = split_index((full, outn * rows), 1, rows)
    wot[...] = jnp.where(ta == tb, dot_nt(spread, lines), 0.0).astype(BF16)

    pl.semaphore_wait(
        barrier, peers - 1 + has_up.astype(jnp.int32) + has_dn.astype(jnp.int32)
    )

    def halo_copies(m, src, dst, send, recv):
        to_up = pltpu.make_async_remote_copy(
            src_ref=src.at[m, 0], dst_ref=dst.at[m, 1], send_sem=send.at[m, 0],
            recv_sem=recv.at[m, 1], device_id=up, device_id_type=MESH,
        )
        to_dn = pltpu.make_async_remote_copy(
            src_ref=src.at[m, 1], dst_ref=dst.at[m, 0], send_sem=send.at[m, 1],
            recv_sem=recv.at[m, 0], device_id=dn, device_id_type=MESH,
        )
        return to_up, to_dn

    def halo_start(m, src, dst, send, recv):
        to_up, to_dn = halo_copies(m, src, dst, send, recv)

        @pl.when(has_up)
        def _():
            to_up.start()

        @pl.when(has_dn)
        def _():
            to_dn.start()

        @pl.when(jnp.logical_not(has_up))
        def _():
            dst[m, 0] = jnp.zeros((chans, cols), BF16)

        @pl.when(jnp.logical_not(has_dn))
        def _():
            dst[m, 1] = jnp.zeros((chans, cols), BF16)

    def halo_wait(m, src, dst, send, recv, which):
        to_up, to_dn = halo_copies(m, src, dst, send, recv)

        @pl.when(has_up)
        def _():
            to_up.wait_send() if which == "send" else to_dn.wait_recv()

        @pl.when(has_dn)
        def _():
            to_dn.wait_send() if which == "send" else to_up.wait_recv()

    def send_edges(m, source, store, dst, send, recv):
        edge = dot(sel[...], source).astype(BF16)
        store[m, 0] = edge[:chans]
        store[m, 1] = edge[chans:]
        halo_start(m, store, dst, send, recv)

    def stack_halo(m, halo, order):
        both = jnp.concatenate([halo[m, 0], halo[m, 1]], axis=0)
        for slot, step in enumerate(order):
            value = both if step == 0 else shifted(both, step)
            hstk[m, slot * 2 * chans : (slot + 1) * 2 * chans, :] = value

    def stack_main(m, value, order):
        for slot, step in enumerate(order):
            stk[m, slot * full : (slot + 1) * full, :] = value if step == 0 else shifted(value, step)

    spans = [slice(n, n + chunk) for n in range(0, cols, chunk)]

    for m in range(members):
        loads[m].wait()
        send_edges(m, x[m], hs, hx, hs_sem, hx_sem)
    for m in range(members):
        stack_main(m, x[m], (-1, 0, 1))
        skips[m].wait()
        for span in spans:
            pre[m, :, span] = dot(wf[...], stk[m, :, span]) + skip[m, :, span].astype(F32)

    def scatter_copy(m, d):
        peer = lax.rem(me + d, peers)
        return pltpu.make_async_remote_copy(
            src_ref=outs.at[m, :, pl.ds(pl.multiple_of(peer * wide, wide), wide)],
            dst_ref=ybuf.at[d, m],
            send_sem=as_sem.at[m, d], recv_sem=ar_sem.at[m, d],
            device_id={"member": peer}, device_id_type=MESH,
        )

    def return_copy(d):
        peer = lax.rem(me + peers - d, peers)
        return pltpu.make_async_remote_copy(
            src_ref=gsend.at[d],
            dst_ref=gout.at[:, :, mine],
            send_sem=bs_sem.at[d], recv_sem=br_sem.at[d],
            device_id={"member": peer}, device_id_type=MESH,
        )

    for m in range(members):
        halo_wait(m, hs, hx, hs_sem, hx_sem, "recv")
        stack_halo(m, hx, (-1, 0, 1))
        for span in spans:
            total = pre[m, :, span] + dot(wfh[...], hstk[m, :, span])
            pre[m, :, span] = total
            outs[m, :, span] = dot(wo[...], gelu_value(total).astype(BF16))
        for d in range(1, peers):
            scatter_copy(m, d).start()
    for m in range(members):
        for span in spans:
            pre[m, :, span] = gelu_slope(pre[m, :, span])
    build(wb, wbh, True)

    tgt.wait()
    for m in range(members):
        for d in range(1, peers):
            scatter_copy(m, d).wait_recv()
    goal = target[...]
    values = []
    for d in range(peers):
        for m in range(members):
            values.append(outs[m, :, mine] if d == 0 else ybuf[d, m])
    total_members = len(values)
    pairs = [smooth_slope(v - v) for v in values]
    for i in range(total_members):
        for j in range(i):
            term = smooth_slope(values[i] - values[j])
            pairs[i] = pairs[i] + term
            pairs[j] = pairs[j] - term
    grads = [
        (smooth_slope(values[i] - goal) - pairs[i] / (total_members - 1)).astype(BF16)
        for i in range(total_members)
    ]
    for d in range(peers):
        for m in range(members):
            grad = grads[d * members + m]
            if d == 0:
                gout[m, :, mine] = grad
            else:
                gsend[d, m] = grad
        if d > 0:
            return_copy(d).start()
    for d in range(1, peers):
        return_copy(d).wait_recv()

    for m in range(members):
        for span in spans:
            grad = dot(wot[...], gout[m, :, span])
            act[m, :, span] = (grad * pre[m, :, span]).astype(BF16)
        send_edges(m, act[m], gs, hg, gs_sem, hg_sem)
    for m in range(members):
        stack_main(m, act[m], (1, 0, -1))
        for span in spans:
            pre[m, :, span] = dot(wb[...], stk[m, :, span])
    for m in range(members):
        halo_wait(m, gs, hg, gs_sem, hg_sem, "recv")
        stack_halo(m, hg, (1, 0, -1))
        for span in spans:
            obuf[m, :, span] = (pre[m, :, span] + dot(wbh[...], hstk[m, :, span])).astype(BF16)
        pltpu.make_async_copy(obuf.at[m], out_hbm.at[m], out_sem.at[m]).start()

    for m in range(members):
        halo_wait(m, hs, hx, hs_sem, hx_sem, "send")
        halo_wait(m, gs, hg, gs_sem, hg_sem, "send")
        for d in range(1, peers):
            scatter_copy(m, d).wait_send()
    for d in range(1, peers):
        return_copy(d).wait_send()
    for m in range(members):
        pltpu.make_async_copy(obuf.at[m], out_hbm.at[m], out_sem.at[m]).wait()


def local(features, skip, conv_weight, out_weight, target):
    members, chans, rows, cols = features.shape
    outn = out_weight.shape[0]
    peers = lax.axis_size("member")
    count = lax.axis_size("space")
    full = chans * rows
    wide = cols // peers
    chunk = min(cols, 256)
    dims = (members, chans, rows, cols, peers, count, outn, chunk)
    dma = pltpu.SemaphoreType.DMA
    anywhere = pl.BlockSpec(memory_space=pl.ANY)
    vmem = pl.BlockSpec(memory_space=pltpu.VMEM)
    result = pl.pallas_call(
        functools.partial(kernel, dims),
        out_shape=jax.ShapeDtypeStruct((members, full, cols), BF16),
        in_specs=[anywhere, anywhere, vmem, vmem, anywhere],
        out_specs=anywhere,
        scratch_shapes=[
            pltpu.VMEM((members, full, cols), BF16),
            pltpu.VMEM((members, full, cols), BF16),
            pltpu.VMEM((outn * rows, wide), F32),
            pltpu.VMEM((members, 3 * full, cols), BF16),
            pltpu.VMEM((members, 6 * chans, cols), BF16),
            pltpu.VMEM((members, full, cols), F32),
            pltpu.VMEM((members, full, cols), BF16),
            pltpu.VMEM((members, 2, chans, cols), BF16),
            pltpu.VMEM((members, 2, chans, cols), BF16),
            pltpu.VMEM((members, 2, chans, cols), BF16),
            pltpu.VMEM((members, 2, chans, cols), BF16),
            pltpu.VMEM((members, outn * rows, cols), F32),
            pltpu.VMEM((peers, members, outn * rows, wide), F32),
            pltpu.VMEM((peers, members, outn * rows, wide), BF16),
            pltpu.VMEM((members, outn * rows, cols), BF16),
            pltpu.VMEM((full, 3 * full), BF16),
            pltpu.VMEM((full, 6 * chans), BF16),
            pltpu.VMEM((full, 3 * full), BF16),
            pltpu.VMEM((full, 6 * chans), BF16),
            pltpu.VMEM((outn * rows, full), BF16),
            pltpu.VMEM((full, outn * rows), BF16),
            pltpu.VMEM((2 * chans, full), BF16),
            pltpu.VMEM((members, full, cols), BF16),
            dma((2 * members + 1,)),
            dma((members,)),
            dma((members, 2)),
            dma((members, 2)),
            dma((members, 2)),
            dma((members, 2)),
            dma((members, peers)),
            dma((members, peers)),
            dma((peers,)),
            dma((peers,)),
        ],
        compiler_params=pltpu.CompilerParams(collective_id=0, has_side_effects=True),
    )(
        features.reshape(members, full, cols),
        skip.reshape(members, full, cols),
        conv_weight,
        out_weight,
        target.reshape(outn * rows, cols),
    )
    return result.reshape(members, chans, rows, cols)


def solution(mesh):
    placed = (
        P("member", None, "space", None),
        P("member", None, "space", None),
        P(),
        P(),
        P(None, "space", None),
    )
    return jax.shard_map(
        local,
        mesh=mesh,
        in_specs=placed,
        out_specs=P("member", None, "space", None),
        check_vma=False,
    )
```

time: 48.4 us -> 24.6 us (0.51)
  Pallas kernels: 0 us -> 22.2 us
  starting transfers between devices: 13.9 us -> 0 us
  blocking collectives: 8.22 us -> 0 us
  matrix products: 7.85 us -> 0 us
  local copies, waits for them, and re-layouts: 9.96 us -> 2.26 us
  waiting for transfers between devices: 5.6 us -> 0 us
  other arithmetic: 2.16 us -> 0 us
    pallas_call x0 -> x1, Pallas kernels: none -> 22.2 us  [local(): pl.pallas_call(functools.partial(kernel, dims), out_shape=jax.ShapeDtypeS...]
    ppermute x4 -> x0, starting transfers between devices: 13.9 us -> none  [the longest x2 9.87 us: extended(): lax.ppermute(tail, axis, [(i, (i + 1) % count) for i in range(ends)])]
    all_gather x1 -> x0, blocking collectives: 8.22 us -> none  [local(): all_members = lax.all_gather(outputs, 'member', axis=0, tiled=True)]
    dot_general x6 -> x0, matrix products: 7.85 us -> none  [the longest x4 4.69 us: tap_sum(): jnp.einsum('ok,krw->orw', matrix, stacked, preferred_element_type=jnp.flo...]
    ppermute x4 -> x0, waiting for transfers between devices: 5.6 us -> none  [the longest x2 5.6 us: extended(): lax.ppermute(head, axis, [((i + 1) % count, i) for i in range(ends)])]
    unnamed x29 -> x1, local copies, waits for them, and re-layouts: 6.47 us -> 2.26 us
    concatenate x2 -> x0, other arithmetic: 1.64 us -> none  [extended(): jnp.concatenate([lax.ppermute(tail, axis, [(i, (i + 1) % count) for i in...]
    another operation x1 -> x0, local copies, waits for them, and re-layouts: 1.55 us -> none  [tap_sum(): return jnp.stack(results, axis=0)]
  transfers between devices with their start and end apart: 4 -> 0, of which waited for: 2 -> 0; matrix products, arithmetic and copies ran while one was open for 6% -> 0% of each run, Pallas kernels for 0% -> 0%
where the time goes in v1:
time: 24.6 us; the launch traced here: 24.4 us
  Pallas kernels  22.2 us (90%)
  local copies, waits for them, and re-layouts  2.26 us (9%)
    pallas_call x1, Pallas kernels, local(): pl.pallas_call(functools.partial(kernel, dims), out_shape=jax.ShapeDtypeS...  22.2 us
    unnamed x1, local copies, waits for them, and re-layouts  2.26 us

profile of v1, /device:TPU:1, one launch (start us, length us, event | category | flops | bytes accessed | tf_op | source)
XLA Modules:
  0.0 24.4 jit_solution(11086327317429683554)
XLA Ops:
  0.0 22.2 %shard_map.55 = bf16[2,256,1024]{2,1,0:T(8,128)(2,1)} custom-call(bf16[2,256,1024]{2,1,0:T(8,128)(2,1)} %bitcast.5, bf16[2,256,1024]{2,1,0:T(8,128)(2,1)} %bitcast.6, bf16[3,3,32,32]{3,2,1,0:T(8,128)(2,1)} %weight.1, bf16[2,32]{1,0:T(2,128)(2,1)} %out_w.1, f32[16,1024]{1,0:T(8,128)} %bitcast.7), custom_call_target="tpu_custom_call" | custom-call | tf_op jit(solution)/shard_map/pallas_call | solution.py:325
  22.2 2.3 %copy.7 = bf16[2,32,8,1024]{3,2,1,0:T(8,128)(2,1)} copy(bf16[2,32,8,1024]{3,2,1,0:T(8,128)(2,1)} %bitcast.4) | data formatting | bytes 2097152

commit v2 on v1

--- a/solution.py
+++ b/solution.py
@@ -16,17 +16,19 @@
 BF16 = jnp.bfloat16
 
 
+def gelu_half(source, square):
+    return 0.5 + 0.5 * jnp.tanh(source * (root_coef + (root_coef * cubic_coef) * square))
+
+
 def gelu_value(source):
-    inside = root_coef * (source + cubic_coef * source * source * source)
-    return 0.5 * source * (1.0 + jnp.tanh(inside))
+    return source * gelu_half(source, source * source)
 
 
 def gelu_slope(source):
     square = source * source
-    tanh_val = jnp.tanh(root_coef * (source + cubic_coef * square * source))
-    return 0.5 * (1.0 + tanh_val) + 0.5 * source * (1.0 - tanh_val * tanh_val) * (
-        root_coef * (1.0 + 3.0 * cubic_coef * square)
-    )
+    half = gelu_half(source, square)
+    rate = 2.0 * root_coef + (6.0 * root_coef * cubic_coef) * square
+    return half + (source * half) * ((1.0 - half) * rate)
 
 
 def smooth_slope(source):
@@ -57,10 +59,10 @@
 
 
 def kernel(
-    dims, x_hbm, skip_hbm, weight, out_w, target_hbm, out_hbm,
+    dims, x_hbm, skip_hbm, weight, out_w, target_hbm, out,
     x, skip, target, stk, hstk, pre, act, hs, hx, gs, hg, outs, ybuf, gsend, gout,
-    wf, wfh, wb, wbh, wo, wot, sel, obuf,
-    in_sem, out_sem, hs_sem, hx_sem, gs_sem, hg_sem, as_sem, ar_sem, bs_sem, br_sem,
+    wf, wfh, wb, wbh, wo, wot, sel,
+    in_sem, hs_sem, hx_sem, gs_sem, hg_sem, as_sem, ar_sem, bs_sem, br_sem,
 ):
     members, chans, rows, cols, peers, count, outn, chunk = dims
     full = chans * rows
@@ -133,6 +135,72 @@
             main[:, dc * full : (dc + 1) * full] = band.astype(BF16)
         halo[...] = edges.astype(BF16)
 
+    pl.semaphore_wait(
+        barrier, peers - 1 + has_up.astype(jnp.int32) + has_dn.astype(jnp.int32)
+    )
+
+    def halo_copies(m, src, dst, send, recv):
+        to_up = pltpu.make_async_remote_copy(
+            src_ref=src.at[m, 0], dst_ref=dst.at[m, 1], send_sem=send.at[m, 0],
+            recv_sem=recv.at[m, 1], device_id=up, device_id_type=MESH,
+        )
+        to_dn = pltpu.make_async_remote_copy(
+            src_ref=src.at[m, 1], dst_ref=dst.at[m, 0], send_sem=send.at[m, 1],
+            recv_sem=recv.at[m, 0], device_id=dn, device_id_type=MESH,
+        )
+        return to_up, to_dn
+
+    def halo_start(m, src, dst, send, recv):
+        to_up, to_dn = halo_copies(m, src, dst, send, recv)
+
+        @pl.when(has_up)
+        def _():
+            to_up.start()
+
+        @pl.when(has_dn)
+        def _():
+            to_dn.start()
+
+        @pl.when(jnp.logical_not(has_up))
+        def _():
+            dst[m, 0] = jnp.zeros((chans, cols), BF16)
+
+        @pl.when(jnp.logical_not(has_dn))
+        def _():
+            dst[m, 1] = jnp.zeros((chans, cols), BF16)
+
+    def halo_wait(m, src, dst, send, recv, which):
+        to_up, to_dn = halo_copies(m, src, dst, send, recv)
+
+        @pl.when(has_up)
+        def _():
+            to_up.wait_send() if which == "send" else to_dn.wait_recv()
+
+        @pl.when(has_dn)
+        def _():
+            to_dn.wait_send() if which == "send" else to_up.wait_recv()
+
+    def send_edges(m, source, store, dst, send, recv):
+        edge = dot(sel[...], source).astype(BF16)
+        store[m, 0] = edge[:chans]
+        store[m, 1] = edge[chans:]
+        halo_start(m, store, dst, send, recv)
+
+    def stack_halo(m, halo, order):
+        both = jnp.concatenate([halo[m, 0], halo[m, 1]], axis=0)
+        for slot, step in enumerate(order):
+            value = both if step == 0 else shifted(both, step)
+            hstk[m, slot * 2 * chans : (slot + 1) * 2 * chans, :] = value
+
+    def stack_main(m, value, order):
+        for slot, step in enumerate(order):
+            stk[m, slot * full : (slot + 1) * full, :] = value if step == 0 else shifted(value, step)
+
+    spans = [slice(n, n + chunk) for n in range(0, cols, chunk)]
+
+    for m in range(members):
+        loads[m].wait()
+        send_edges(m, x[m], hs, hx, hs_sem, hx_sem)
     build(wf, wfh, False)
 
     out_k, _ = split_index((outn * rows, chans), 0, rows)
@@ -146,73 +214,6 @@
     _, ta = split_index((full, outn * rows), 0, rows)
     _, tb = split_index((full, outn * rows), 1, rows)
     wot[...] = jnp.where(ta == tb, dot_nt(spread, lines), 0.0).astype(BF16)
-
-    pl.semaphore_wait(
-        barrier, peers - 1 + has_up.astype(jnp.int32) + has_dn.astype(jnp.int32)
-    )
-
-    def halo_copies(m, src, dst, send, recv):
-        to_up = pltpu.make_async_remote_copy(
-            src_ref=src.at[m, 0], dst_ref=dst.at[m, 1], send_sem=send.at[m, 0],
-            recv_sem=recv.at[m, 1], device_id=up, device_id_type=MESH,
-        )
-        to_dn = pltpu.make_async_remote_copy(
-            src_ref=src.at[m, 1], dst_ref=dst.at[m, 0], send_sem=send.at[m, 1],
-            recv_sem=recv.at[m, 0], device_id=dn, device_id_type=MESH,
-        )
-        return to_up, to_dn
-
-    def halo_start(m, src, dst, send, recv):
-        to_up, to_dn = halo_copies(m, src, dst, send, recv)
-
-        @pl.when(has_up)
-        def _():
-            to_up.start()
-
-        @pl.when(has_dn)
-        def _():
-            to_dn.start()
-
-        @pl.when(jnp.logical_not(has_up))
-        def _():
-            dst[m, 0] = jnp.zeros((chans, cols), BF16)
-
-        @pl.when(jnp.logical_not(has_dn))
-        def _():
-            dst[m, 1] = jnp.zeros((chans, cols), BF16)
-
-    def halo_wait(m, src, dst, send, recv, which):
-        to_up, to_dn = halo_copies(m, src, dst, send, recv)
-
-        @pl.when(has_up)
-        def _():
-            to_up.wait_send() if which == "send" else to_dn.wait_recv()
-
-        @pl.when(has_dn)
-        def _():
-            to_dn.wait_send() if which == "send" else to_up.wait_recv()
-
-    def send_edges(m, source, store, dst, send, recv):
-        edge = dot(sel[...], source).astype(BF16)
-        store[m, 0] = edge[:chans]
-        store[m, 1] = edge[chans:]
-        halo_start(m, store, dst, send, recv)
-
-    def stack_halo(m, halo, order):
-        both = jnp.concatenate([halo[m, 0], halo[m, 1]], axis=0)
-        for slot, step in enumerate(order):
-            value = both if step == 0 else shifted(both, step)
-            hstk[m, slot * 2 * chans : (slot + 1) * 2 * chans, :] = value
-
-    def stack_main(m, value, order):
-        for slot, step in enumerate(order):
-            stk[m, slot * full : (slot + 1) * full, :] = value if step == 0 else shifted(value, step)
-
-    spans = [slice(n, n + chunk) for n in range(0, cols, chunk)]
-
-    for m in range(members):
-        loads[m].wait()
-        send_edges(m, x[m], hs, hx, hs_sem, hx_sem)
     for m in range(members):
         stack_main(m, x[m], (-1, 0, 1))
         skips[m].wait()
@@ -249,8 +250,6 @@
     for m in range(members):
         for span in spans:
             pre[m, :, span] = gelu_slope(pre[m, :, span])
-    build(wb, wbh, True)
-
     tgt.wait()
     for m in range(members):
         for d in range(1, peers):
@@ -280,6 +279,7 @@
                 gsend[d, m] = grad
         if d > 0:
             return_copy(d).start()
+    build(wb, wbh, True)
     for d in range(1, peers):
         return_copy(d).wait_recv()
 
@@ -296,8 +296,7 @@
         halo_wait(m, gs, hg, gs_sem, hg_sem, "recv")
         stack_halo(m, hg, (1, 0, -1))
         for span in spans:
-            obuf[m, :, span] = (pre[m, :, span] + dot(wbh[...], hstk[m, :, span])).astype(BF16)
-        pltpu.make_async_copy(obuf.at[m], out_hbm.at[m], out_sem.at[m]).start()
+            out[m, :, span] = (pre[m, :, span] + dot(wbh[...], hstk[m, :, span])).astype(BF16)
 
     for m in range(members):
         halo_wait(m, hs, hx, hs_sem, hx_sem, "send")
@@ -306,8 +305,6 @@
             scatter_copy(m, d).wait_send()
     for d in range(1, peers):
         return_copy(d).wait_send()
-    for m in range(members):
-        pltpu.make_async_copy(obuf.at[m], out_hbm.at[m], out_sem.at[m]).wait()
 
 
 def local(features, skip, conv_weight, out_weight, target):
@@ -320,13 +317,13 @@
     chunk = min(cols, 256)
     dims = (members, chans, rows, cols, peers, count, outn, chunk)
     dma = pltpu.SemaphoreType.DMA
-    anywhere = pl.BlockSpec(memory_space=pl.ANY)
+    anywhere = pl.BlockSpec(memory_space=pltpu.HBM)
     vmem = pl.BlockSpec(memory_space=pltpu.VMEM)
     result = pl.pallas_call(
         functools.partial(kernel, dims),
-        out_shape=jax.ShapeDtypeStruct((members, full, cols), BF16),
+        out_shape=pltpu.VMEM((members, full, cols), BF16),
         in_specs=[anywhere, anywhere, vmem, vmem, anywhere],
-        out_specs=anywhere,
+        out_specs=vmem,
         scratch_shapes=[
             pltpu.VMEM((members, full, cols), BF16),
             pltpu.VMEM((members, full, cols), BF16),
@@ -350,9 +347,7 @@
             pltpu.VMEM((outn * rows, full), BF16),
             pltpu.VMEM((full, outn * rows), BF16),
             pltpu.VMEM((2 * chans, full), BF16),
-            pltpu.VMEM((members, full, cols), BF16),
             dma((2 * members + 1,)),
-            dma((members,)),
             dma((members, 2)),
             dma((members, 2)),
             dma((members, 2)),
@@ -362,7 +357,7 @@
             dma((peers,)),
             dma((peers,)),
         ],
-        compiler_params=pltpu.CompilerParams(collective_id=0, has_side_effects=True),
+        compiler_params=pltpu.CompilerParams(collective_id=0, has_side_effects=True, vmem_limit_bytes=58 * 2**20),
     )(
         features.reshape(members, full, cols),
         skip.reshape(members, full, cols),

time: 24.6 us -> 23.2 us (0.943)
  local copies, waits for them, and re-layouts: 2.26 us -> 0.97 us
    unnamed x1, local copies, waits for them, and re-layouts: 2.26 us -> 0.97 us
where the time goes in v2:
time: 23.2 us; the launch traced here: 23.1 us
  Pallas kernels  22.1 us (95%)
  local copies, waits for them, and re-layouts  0.97 us (4%)
    pallas_call x1, Pallas kernels, local(): pl.pallas_call(functools.partial(kernel, dims), out_shape=pltpu.VMEM((mem...  22.1 us
    unnamed x1, local copies, waits for them, and re-layouts  0.97 us

profile of v2, /device:TPU:1, one launch (start us, length us, event | category | flops | bytes accessed | tf_op | source)
XLA Modules:
  0.0 23.1 jit_solution(4974810112355579972)
XLA Ops:
  0.0 22.1 %shard_map.55 = bf16[2,256,1024]{2,1,0:T(8,128)(2,1)S(1)} custom-call(bf16[2,256,1024]{2,1,0:T(8,128)(2,1)} %bitcast.5, bf16[2,256,1024]{2,1,0:T(8,128)(2,1)} %bitcast.6, bf16[3,3,32,32]{3,2,1,0:T(8,128)(2,1)} %weight.1, bf16[2,32]{1,0:T(2,128)(2,1)} %out_w.1, f32[16,1024]{1,0:T(8,128)} %bitcast.7), custom_call_target="tpu_custom_call" | custom-call | tf_op jit(solution)/shard_map/pallas_call | solution.py:322
  22.1 1.0 %copy.7 = bf16[2,32,8,1024]{3,2,1,0:T(8,128)(2,1)} copy(bf16[2,32,8,1024]{3,2,1,0:T(8,128)(2,1)S(1)} %bitcast.4) | data formatting | bytes 2097152

commit v3 on v2

--- a/solution.py
+++ b/solution.py
@@ -11,6 +11,7 @@
 root_coef = math.sqrt(2.0 / math.pi)
 cubic_coef = 0.044715
 smooth = 0.25
+lane = 128
 MESH = pl.DeviceIdType.MESH
 F32 = jnp.float32
 BF16 = jnp.bfloat16
@@ -60,27 +61,25 @@
 
 def kernel(
     dims, x_hbm, skip_hbm, weight, out_w, target_hbm, out,
-    x, skip, target, stk, hstk, pre, act, hs, hx, gs, hg, outs, ybuf, gsend, gout,
+    x, skip, target, stk, hstk, pre, act, hs, hx, gs, hg, outs, osend, ybuf, gout, se, woe,
     wf, wfh, wb, wbh, wo, wot, sel,
-    in_sem, hs_sem, hx_sem, gs_sem, hg_sem, as_sem, ar_sem, bs_sem, br_sem,
+    in_sem, hs_sem, hx_sem, gs_sem, hg_sem, as_sem, ar_sem,
 ):
     members, chans, rows, cols, peers, count, outn, chunk = dims
     full = chans * rows
-    wide = cols // peers
     me = lax.axis_index("member")
     at = lax.axis_index("space")
     has_up = at > 0
     has_dn = at < count - 1
     up = {"space": lax.max(at - 1, 0)}
     dn = {"space": lax.min(at + 1, count - 1)}
-    mine = pl.ds(pl.multiple_of(me * wide, wide), wide)
 
     loads = [pltpu.make_async_copy(x_hbm.at[m], x.at[m], in_sem.at[m]) for m in range(members)]
     skips = [
         pltpu.make_async_copy(skip_hbm.at[m], skip.at[m], in_sem.at[members + m])
         for m in range(members)
     ]
-    tgt = pltpu.make_async_copy(target_hbm.at[:, mine], target, in_sem.at[2 * members])
+    tgt = pltpu.make_async_copy(target_hbm, target, in_sem.at[2 * members])
     for c in loads + skips + [tgt]:
         c.start()
 
@@ -123,16 +122,19 @@
         for dc in range(3):
             band = jnp.zeros((full, full), F32)
             for dr in range(3):
-                tap = weight[dr, dc]
-                part = (dot_nt if flipped else dot)(spread, tap).astype(BF16)
                 offset = 1 - dr if flipped else dr - 1
-                band = jnp.where(gap == offset, dot_nt(part, spread), band)
+                if flipped and offset == 0:
+                    continue
+                part = (dot_nt if flipped else dot)(spread, weight[dr, dc]).astype(BF16)
+                if not flipped:
+                    band = jnp.where(gap == offset, dot_nt(part, spread), band)
                 if offset != 0:
                     kept = jnp.where(
                         left_row == (0 if offset < 0 else rows - 1), part.astype(F32), 0.0
                     ).astype(BF16)
                     edges = edges + dot(kept, place(2 * dc + (0 if offset < 0 else 1)))
-            main[:, dc * full : (dc + 1) * full] = band.astype(BF16)
+            span = slice(dc * full, (dc + 1) * full)
+            main[:, span] = wf[:, span].T if flipped else band.astype(BF16)
         halo[...] = edges.astype(BF16)
 
     pl.semaphore_wait(
@@ -197,6 +199,14 @@
             stk[m, slot * full : (slot + 1) * full, :] = value if step == 0 else shifted(value, step)
 
     spans = [slice(n, n + chunk) for n in range(0, cols, chunk)]
+
+    def get(m, span, lines=slice(None)):
+        tiles = range(span.start // lane, span.stop // lane)
+        return jnp.concatenate([pre[m, tile, lines, :] for tile in tiles], axis=1)
+
+    def put(m, span, value, lines=slice(None)):
+        for k, tile in enumerate(range(span.start // lane, span.stop // lane)):
+            pre[m, tile, lines, :] = value[:, k * lane : (k + 1) * lane]
 
     for m in range(members):
         loads[m].wait()
@@ -218,93 +228,94 @@
         stack_main(m, x[m], (-1, 0, 1))
         skips[m].wait()
         for span in spans:
-            pre[m, :, span] = dot(wf[...], stk[m, :, span]) + skip[m, :, span].astype(F32)
-
-    def scatter_copy(m, d):
-        peer = lax.rem(me + d, peers)
+            put(m, span, dot(wf[...], stk[m, :, span]) + skip[m, :, span].astype(F32))
+
+    parts = [slice(n, n + cols // 2) for n in range(0, cols, cols // 2)]
+
+    def gather_copy(m, part, d):
         return pltpu.make_async_remote_copy(
-            src_ref=outs.at[m, :, pl.ds(pl.multiple_of(peer * wide, wide), wide)],
-            dst_ref=ybuf.at[d, m],
-            send_sem=as_sem.at[m, d], recv_sem=ar_sem.at[m, d],
-            device_id={"member": peer}, device_id_type=MESH,
-        )
-
-    def return_copy(d):
-        peer = lax.rem(me + peers - d, peers)
-        return pltpu.make_async_remote_copy(
-            src_ref=gsend.at[d],
-            dst_ref=gout.at[:, :, mine],
-            send_sem=bs_sem.at[d], recv_sem=br_sem.at[d],
-            device_id={"member": peer}, device_id_type=MESH,
+            src_ref=osend.at[m, :, parts[part]],
+            dst_ref=ybuf.at[d, m, :, parts[part]],
+            send_sem=as_sem.at[m, part, d], recv_sem=ar_sem.at[m, part, d],
+            device_id={"member": lax.rem(me + d, peers)}, device_id_type=MESH,
         )
 
     for m in range(members):
         halo_wait(m, hs, hx, hs_sem, hx_sem, "recv")
         stack_halo(m, hx, (-1, 0, 1))
-        for span in spans:
-            total = pre[m, :, span] + dot(wfh[...], hstk[m, :, span])
-            pre[m, :, span] = total
-            outs[m, :, span] = dot(wo[...], gelu_value(total).astype(BF16))
+        for part, range_of in enumerate(parts):
+            for n in range(range_of.start, range_of.stop, chunk):
+                span = slice(n, n + chunk)
+                total = get(m, span) + dot(wfh[...], hstk[m, :, span])
+                put(m, span, total)
+                value = dot(wo[...], gelu_value(total).astype(BF16))
+                outs[m, :, span] = value
+                osend[m, :, span] = value.astype(BF16)
+            for d in range(1, peers):
+                gather_copy(m, part, d).start()
+    block = 8 * rows
+    for m in range(members):
+        for n in range(0, full, block):
+            for span in spans:
+                lines = slice(n, n + block)
+                put(m, span, gelu_slope(get(m, span, lines)), lines)
+        for half in range(2):
+            for tile in range(cols // lane):
+                kept = pre[m, tile, pl.ds(half * (rows - 1), chans, stride=rows), :]
+                se[m, half, :, tile * lane : (tile + 1) * lane] = kept
+    build(wb, wbh, True)
+    woe[...] = dot(sel[...], wot[...]).astype(BF16)
+
+    tgt.wait()
+    total_members = peers * members
+    for part in range(2):
         for d in range(1, peers):
-            scatter_copy(m, d).start()
-    for m in range(members):
-        for span in spans:
-            pre[m, :, span] = gelu_slope(pre[m, :, span])
-    tgt.wait()
-    for m in range(members):
-        for d in range(1, peers):
-            scatter_copy(m, d).wait_recv()
-    goal = target[...]
-    values = []
-    for d in range(peers):
-        for m in range(members):
-            values.append(outs[m, :, mine] if d == 0 else ybuf[d, m])
-    total_members = len(values)
-    pairs = [smooth_slope(v - v) for v in values]
-    for i in range(total_members):
-        for j in range(i):
-            term = smooth_slope(values[i] - values[j])
-            pairs[i] = pairs[i] + term
-            pairs[j] = pairs[j] - term
-    grads = [
-        (smooth_slope(values[i] - goal) - pairs[i] / (total_members - 1)).astype(BF16)
-        for i in range(total_members)
-    ]
-    for d in range(peers):
-        for m in range(members):
-            grad = grads[d * members + m]
-            if d == 0:
-                gout[m, :, mine] = grad
-            else:
-                gsend[d, m] = grad
-        if d > 0:
-            return_copy(d).start()
-    build(wb, wbh, True)
-    for d in range(1, peers):
-        return_copy(d).wait_recv()
-
+            for m in range(members):
+                gather_copy(m, part, d).wait_recv()
+        for n in range(parts[part].start, parts[part].stop, chunk):
+            span = slice(n, n + chunk)
+            own = [outs[m, :, span] for m in range(members)]
+            pairs = [smooth_slope(v - v) for v in own]
+            for i in range(members):
+                for j in range(i):
+                    term = smooth_slope(own[i] - own[j])
+                    pairs[i] = pairs[i] + term
+                    pairs[j] = pairs[j] - term
+            for d in range(1, peers):
+                for j in range(members):
+                    other = ybuf[d, j, :, span].astype(F32)
+                    for i in range(members):
+                        pairs[i] = pairs[i] + smooth_slope(own[i] - other)
+            for i in range(members):
+                gout[i, :, span] = (
+                    smooth_slope(own[i] - target[:, span]) - pairs[i] / (total_members - 1)
+                ).astype(BF16)
+
+    for m in range(members):
+        edge = dot(woe[...], gout[m])
+        for half in range(2):
+            gs[m, half] = (edge[half * chans : (half + 1) * chans] * se[m, half]).astype(BF16)
+        halo_start(m, gs, hg, gs_sem, hg_sem)
     for m in range(members):
         for span in spans:
             grad = dot(wot[...], gout[m, :, span])
-            act[m, :, span] = (grad * pre[m, :, span]).astype(BF16)
-        send_edges(m, act[m], gs, hg, gs_sem, hg_sem)
+            act[m, :, span] = (grad * get(m, span)).astype(BF16)
     for m in range(members):
         stack_main(m, act[m], (1, 0, -1))
         for span in spans:
-            pre[m, :, span] = dot(wb[...], stk[m, :, span])
+            put(m, span, dot(wb[...], stk[m, :, span]))
     for m in range(members):
         halo_wait(m, gs, hg, gs_sem, hg_sem, "recv")
         stack_halo(m, hg, (1, 0, -1))
         for span in spans:
-            out[m, :, span] = (pre[m, :, span] + dot(wbh[...], hstk[m, :, span])).astype(BF16)
+            out[m, :, span] = (get(m, span) + dot(wbh[...], hstk[m, :, span])).astype(BF16)
 
     for m in range(members):
         halo_wait(m, hs, hx, hs_sem, hx_sem, "send")
         halo_wait(m, gs, hg, gs_sem, hg_sem, "send")
-        for d in range(1, peers):
-            scatter_copy(m, d).wait_send()
-    for d in range(1, peers):
-        return_copy(d).wait_send()
+        for part in range(2):
+            for d in range(1, peers):
+                gather_copy(m, part, d).wait_send()
 
 
 def local(features, skip, conv_weight, out_weight, target):
@@ -313,7 +324,6 @@
     peers = lax.axis_size("member")
     count = lax.axis_size("space")
     full = chans * rows
-    wide = cols // peers
     chunk = min(cols, 256)
     dims = (members, chans, rows, cols, peers, count, outn, chunk)
     dma = pltpu.SemaphoreType.DMA
@@ -327,19 +337,21 @@
         scratch_shapes=[
             pltpu.VMEM((members, full, cols), BF16),
             pltpu.VMEM((members, full, cols), BF16),
-            pltpu.VMEM((outn * rows, wide), F32),
+            pltpu.VMEM((outn * rows, cols), F32),
             pltpu.VMEM((members, 3 * full, cols), BF16),
             pltpu.VMEM((members, 6 * chans, cols), BF16),
-            pltpu.VMEM((members, full, cols), F32),
+            pltpu.VMEM((members, cols // lane, full, lane), F32),
             pltpu.VMEM((members, full, cols), BF16),
             pltpu.VMEM((members, 2, chans, cols), BF16),
             pltpu.VMEM((members, 2, chans, cols), BF16),
             pltpu.VMEM((members, 2, chans, cols), BF16),
             pltpu.VMEM((members, 2, chans, cols), BF16),
             pltpu.VMEM((members, outn * rows, cols), F32),
-            pltpu.VMEM((peers, members, outn * rows, wide), F32),
-            pltpu.VMEM((peers, members, outn * rows, wide), BF16),
             pltpu.VMEM((members, outn * rows, cols), BF16),
+            pltpu.VMEM((peers, members, outn * rows, cols), BF16),
+            pltpu.VMEM((members, outn * rows, cols), BF16),
+            pltpu.VMEM((members, 2, chans, cols), F32),
+            pltpu.VMEM((2 * chans, outn * rows), BF16),
             pltpu.VMEM((full, 3 * full), BF16),
             pltpu.VMEM((full, 6 * chans), BF16),
             pltpu.VMEM((full, 3 * full), BF16),
@@ -352,10 +364,8 @@
             dma((members, 2)),
             dma((members, 2)),
             dma((members, 2)),
-            dma((members, peers)),
-            dma((members, peers)),
-            dma((peers,)),
-            dma((peers,)),
+            dma((members, 2, peers)),
+            dma((members, 2, peers)),
         ],
         compiler_params=pltpu.CompilerParams(collective_id=0, has_side_effects=True, vmem_limit_bytes=58 * 2**20),
     )(

time: 23.2 us -> 19.5 us (0.84)
  Pallas kernels: 22.1 us -> 18.3 us
    pallas_call x1, Pallas kernels: 22.1 us -> 18.3 us  [local(): pl.pallas_call(functools.partial(kernel, dims), out_shape=pltpu.VMEM((mem...]
where the time goes in v3:
time: 19.5 us; the launch traced here: 19.3 us
  Pallas kernels  18.3 us (94%)
  local copies, waits for them, and re-layouts  0.97 us (5%)
    pallas_call x1, Pallas kernels, local(): pl.pallas_call(functools.partial(kernel, dims), out_shape=pltpu.VMEM((mem...  18.3 us
    unnamed x1, local copies, waits for them, and re-layouts  0.97 us

profile of v3, /device:TPU:1, one launch (start us, length us, event | category | flops | bytes accessed | tf_op | source)
XLA Modules:
  0.0 19.3 jit_solution(11202256781244065467)
XLA Ops:
  0.0 18.3 %shard_map.55 = bf16[2,256,1024]{2,1,0:T(8,128)(2,1)S(1)} custom-call(bf16[2,256,1024]{2,1,0:T(8,128)(2,1)} %bitcast.5, bf16[2,256,1024]{2,1,0:T(8,128)(2,1)} %bitcast.6, bf16[3,3,32,32]{3,2,1,0:T(8,128)(2,1)} %weight.1, bf16[2,32]{1,0:T(2,128)(2,1)} %out_w.1, f32[16,1024]{1,0:T(8,128)} %bitcast.7), custom_call_target="tpu_custom_call" | custom-call | tf_op jit(solution)/shard_map/pallas_call | solution.py:332
  18.3 1.0 %copy.7 = bf16[2,32,8,1024]{3,2,1,0:T(8,128)(2,1)} copy(bf16[2,32,8,1024]{3,2,1,0:T(8,128)(2,1)S(1)} %bitcast.4) | data formatting | bytes 2097152

commit v4 on v3

--- a/solution.py
+++ b/solution.py
@@ -61,9 +61,9 @@
 
 def kernel(
     dims, x_hbm, skip_hbm, weight, out_w, target_hbm, out,
-    x, skip, target, stk, hstk, pre, act, hs, hx, gs, hg, outs, osend, ybuf, gout, se, woe,
+    x, skip, target, stk, hstk, pre, act, hs, hx, hse, hg, hgo, outs, osend, ybuf, gout, se, woe,
     wf, wfh, wb, wbh, wo, wot, sel,
-    in_sem, hs_sem, hx_sem, gs_sem, hg_sem, as_sem, ar_sem,
+    in_sem, hs_sem, hx_sem, gs_sem, hg_sem, as_sem, ar_sem, cs_sem, cr_sem,
 ):
     members, chans, rows, cols, peers, count, outn, chunk = dims
     full = chans * rows
@@ -141,13 +141,16 @@
         barrier, peers - 1 + has_up.astype(jnp.int32) + has_dn.astype(jnp.int32)
     )
 
+    def edge_of(src, m, half):
+        return src.at[m, half] if len(src.shape) == 4 else src.at[m]
+
     def halo_copies(m, src, dst, send, recv):
         to_up = pltpu.make_async_remote_copy(
-            src_ref=src.at[m, 0], dst_ref=dst.at[m, 1], send_sem=send.at[m, 0],
+            src_ref=edge_of(src, m, 0), dst_ref=dst.at[m, 1], send_sem=send.at[m, 0],
             recv_sem=recv.at[m, 1], device_id=up, device_id_type=MESH,
         )
         to_dn = pltpu.make_async_remote_copy(
-            src_ref=src.at[m, 1], dst_ref=dst.at[m, 0], send_sem=send.at[m, 1],
+            src_ref=edge_of(src, m, 1), dst_ref=dst.at[m, 0], send_sem=send.at[m, 1],
             recv_sem=recv.at[m, 0], device_id=dn, device_id_type=MESH,
         )
         return to_up, to_dn
@@ -165,11 +168,11 @@
 
         @pl.when(jnp.logical_not(has_up))
         def _():
-            dst[m, 0] = jnp.zeros((chans, cols), BF16)
+            dst[m, 0] = jnp.zeros(dst.shape[2:], dst.dtype)
 
         @pl.when(jnp.logical_not(has_dn))
         def _():
-            dst[m, 1] = jnp.zeros((chans, cols), BF16)
+            dst[m, 1] = jnp.zeros(dst.shape[2:], dst.dtype)
 
     def halo_wait(m, src, dst, send, recv, which):
         to_up, to_dn = halo_copies(m, src, dst, send, recv)
@@ -263,6 +266,7 @@
             for tile in range(cols // lane):
                 kept = pre[m, tile, pl.ds(half * (rows - 1), chans, stride=rows), :]
                 se[m, half, :, tile * lane : (tile + 1) * lane] = kept
+        halo_start(m, se, hse, gs_sem, hg_sem)
     build(wb, wbh, True)
     woe[...] = dot(sel[...], wot[...]).astype(BF16)
 
@@ -292,10 +296,7 @@
                 ).astype(BF16)
 
     for m in range(members):
-        edge = dot(woe[...], gout[m])
-        for half in range(2):
-            gs[m, half] = (edge[half * chans : (half + 1) * chans] * se[m, half]).astype(BF16)
-        halo_start(m, gs, hg, gs_sem, hg_sem)
+        halo_start(m, gout, hgo, cs_sem, cr_sem)
     for m in range(members):
         for span in spans:
             grad = dot(wot[...], gout[m, :, span])
@@ -305,14 +306,19 @@
         for span in spans:
             put(m, span, dot(wb[...], stk[m, :, span]))
     for m in range(members):
-        halo_wait(m, gs, hg, gs_sem, hg_sem, "recv")
+        halo_wait(m, se, hse, gs_sem, hg_sem, "recv")
+        halo_wait(m, gout, hgo, cs_sem, cr_sem, "recv")
+        for half in range(2):
+            far = woe[(1 - half) * chans : (2 - half) * chans, :]
+            hg[m, half] = (dot(far, hgo[m, half]) * hse[m, half]).astype(BF16)
         stack_halo(m, hg, (1, 0, -1))
         for span in spans:
             out[m, :, span] = (get(m, span) + dot(wbh[...], hstk[m, :, span])).astype(BF16)
 
     for m in range(members):
         halo_wait(m, hs, hx, hs_sem, hx_sem, "send")
-        halo_wait(m, gs, hg, gs_sem, hg_sem, "send")
+        halo_wait(m, se, hse, gs_sem, hg_sem, "send")
+        halo_wait(m, gout, hgo, cs_sem, cr_sem, "send")
         for part in range(2):
             for d in range(1, peers):
                 gather_copy(m, part, d).wait_send()
@@ -344,8 +350,9 @@
             pltpu.VMEM((members, full, cols), BF16),
             pltpu.VMEM((members, 2, chans, cols), BF16),
             pltpu.VMEM((members, 2, chans, cols), BF16),
+            pltpu.VMEM((members, 2, chans, cols), F32),
             pltpu.VMEM((members, 2, chans, cols), BF16),
-            pltpu.VMEM((members, 2, chans, cols), BF16),
+            pltpu.VMEM((members, 2, outn * rows, cols), BF16),
             pltpu.VMEM((members, outn * rows, cols), F32),
             pltpu.VMEM((members, outn * rows, cols), BF16),
             pltpu.VMEM((peers, members, outn * rows, cols), BF16),
@@ -366,6 +373,8 @@
             dma((members, 2)),
             dma((members, 2, peers)),
             dma((members, 2, peers)),
+            dma((members, 2)),
+            dma((members, 2)),
         ],
         compiler_params=pltpu.CompilerParams(collective_id=0, has_side_effects=True, vmem_limit_bytes=58 * 2**20),
     )(

time: 19.5 us -> 19.2 us (0.985)
  Pallas kernels: 18.3 us -> 18.1 us
    pallas_call x1, Pallas kernels: 18.3 us -> 18.1 us  [local(): pl.pallas_call(functools.partial(kernel, dims), out_shape=pltpu.VMEM((mem...]
where the time goes in v4:
time: 19.2 us; the launch traced here: 19.1 us
  Pallas kernels  18.1 us (94%)
  local copies, waits for them, and re-layouts  0.97 us (5%)
    pallas_call x1, Pallas kernels, local(): pl.pallas_call(functools.partial(kernel, dims), out_shape=pltpu.VMEM((mem...  18.1 us
    unnamed x1, local copies, waits for them, and re-layouts  0.97 us

profile of v4, /device:TPU:1, one launch (start us, length us, event | category | flops | bytes accessed | tf_op | source)
XLA Modules:
  0.0 19.1 jit_solution(6089267325969973791)
XLA Ops:
  0.0 18.1 %shard_map.55 = bf16[2,256,1024]{2,1,0:T(8,128)(2,1)S(1)} custom-call(bf16[2,256,1024]{2,1,0:T(8,128)(2,1)} %bitcast.5, bf16[2,256,1024]{2,1,0:T(8,128)(2,1)} %bitcast.6, bf16[3,3,32,32]{3,2,1,0:T(8,128)(2,1)} %weight.1, bf16[2,32]{1,0:T(2,128)(2,1)} %out_w.1, f32[16,1024]{1,0:T(8,128)} %bitcast.7), custom_call_target="tpu_custom_call" | custom-call | tf_op jit(solution)/shard_map/pallas_call | solution.py:338
  18.1 1.0 %copy.7 = bf16[2,32,8,1024]{3,2,1,0:T(8,128)(2,1)} copy(bf16[2,32,8,1024]{3,2,1,0:T(8,128)(2,1)S(1)} %bitcast.4) | data formatting | bytes 2097152
